TPU v7x, 32 devices: a whole 2x2x4 slice. The times are simulated.
32 devices in a mesh: tm: 8 (over z, y), lat: 4 (over x, core).
Axes of the slice: x: 2, y: 2, z: 4, core: 2. Of those that a mesh axis runs over, the one named last changes fastest.
Arguments:
- traj: float32 [8, 83, 24, 192], P('tm', None, 'lat'), may hold values from -6 to 6
- noise: float32 [8, 83, 24, 192], P('tm', None, 'lat'), may hold values from -6 to 6
- step_index: int32 [8], P('tm'), may hold values from 0 to 999
- embed_weight: bfloat16 [83, 512], replicated, may hold values from -0.625 to 0.625
- time_weight: float32 [512, 512], replicated, may hold values from -0.25 to 0.25
- dw_weight: float32 [512, 25], replicated, may hold values from -1.25 to 1.25
- ln_gain: float32 [512], replicated, may hold values from 0.5 to 1.5
- up_weight: bfloat16 [512, 1024], replicated, may hold values from -0.25 to 0.25
- down_weight: bfloat16 [1024, 512], replicated, may hold values from -0.1875 to 0.1875
- out_weight: bfloat16 [512, 83], replicated, may hold values from -0.25 to 0.25
Outputs:
- trajectory: float32 [8, 83, 24, 192], P('tm', None, 'lat')
All inputs are finite; a program needn't handle non-finite values.
Results may differ from a plain program's by a relative error of at most 0.0025.
Values may be sent and summed in bfloat16 or wider, within the bound.
No kernel may reach another device: no remote copies, remote signals or barrier semaphores. Data moves between devices by JAX's collectives and lax.ppermute only.
A program may use at most 128 MiB of HBM per device.

v0:
```python
import math
import jax
import jax.numpy as jnp
from jax import lax
from jax.sharding import PartitionSpec as P

ITERS = 2
LEVELS = 1000


def with_halo(x, sides, width):
    for axis, dim in sides:
        devices, length = (lax.axis_size(axis), x.shape[dim])
        up = [(i, (i + 1) % devices) for i in range(devices - 1)]
        down = [(j, i) for i, j in up]
        last = lax.slice_in_dim(x, length - width, length, axis=dim)
        first = lax.slice_in_dim(x, 0, width, axis=dim)
        before = lax.ppermute(last, axis, up)
        after = lax.ppermute(first, axis, down)
        x = jnp.concatenate([before, x, after], axis=dim)
    return x


def entering(part, axis, combine, identity):
    place = lax.axis_index(axis)
    gathered = lax.all_gather(part, axis)
    state = jnp.zeros_like(part) + jnp.asarray(identity, part.dtype)

    def one(turn, state):
        return combine(state, lax.dynamic_index_in_dim(gathered, turn, 0, False))

    return lax.fori_loop(0, place, one, state)


def spread(value, axis, source):
    kept = jnp.where(lax.axis_index(axis) == source, value, 0).astype(value.dtype)
    return lax.psum(kept, axis)


def noise_levels(step_index):
    log_ratio = math.log(0.1) / (LEVELS - 1)
    return 2.0 * jnp.exp(step_index.astype(jnp.float32) * log_ratio)


def conditions(noise_level, time_weight):
    half_width = time_weight.shape[0] // 2
    frequency = jnp.exp(jnp.arange(half_width, dtype=jnp.float32) * (-math.log(100.0) / half_width))
    angles = jnp.log(noise_level)[:, None] * frequency[None, :]
    features = jnp.concatenate([jnp.cos(angles), jnp.sin(angles)], axis=1)
    return jax.nn.silu(jnp.dot(features, time_weight, precision=lax.Precision.HIGHEST))


def depthwise_taps(lat_padded, dw_weight):
    lat_rows = lat_padded.shape[1] - 4
    widened = lat_padded.astype(jnp.float32)
    lon_cols = widened.shape[2]
    widened = jnp.concatenate([widened[:, :, -2:], widened, widened[:, :, :2]], axis=2)
    summed = jnp.zeros((widened.shape[0], lat_rows, lon_cols), jnp.float32)
    for row_tap in range(5):
        for col_tap in range(5):
            summed = (
                summed
                + dw_weight[:, row_tap * 5 + col_tap][:, None, None]
                * widened[:, row_tap : row_tap + lat_rows, col_tap : col_tap + lon_cols]
            )
    return summed


def denoise(
    current, condition, embed_weight, dw_weight, ln_gain, up_weight, down_weight, out_weight
):
    channels, lat_rows, lon_cols = current.shape
    width = embed_weight.shape[1]
    as_rows = current.astype(jnp.bfloat16).reshape(channels, lat_rows * lon_cols)
    embedded = jnp.dot(embed_weight.T, as_rows, preferred_element_type=jnp.float32)
    activation = (embedded + condition[:, None]).astype(jnp.bfloat16)
    padded = with_halo(activation.reshape(width, lat_rows, lon_cols), (("lat", 1),), 2)
    convolved = depthwise_taps(padded, dw_weight).reshape(width, lat_rows * lon_cols)
    average = jnp.mean(convolved, axis=0)
    centred = convolved - average[None, :]
    variance = jnp.mean(centred * centred, axis=0)
    normed = (centred * lax.rsqrt(variance + 1e-06)[None, :] * ln_gain[:, None]).astype(
        jnp.bfloat16
    )
    hidden = jax.nn.gelu(
        jnp.dot(up_weight.T, normed, preferred_element_type=jnp.float32), approximate=True
    ).astype(jnp.bfloat16)
    block_out = (
        activation.astype(jnp.float32)
        + jnp.dot(down_weight.T, hidden, preferred_element_type=jnp.float32)
    ).astype(jnp.bfloat16)
    return jnp.dot(out_weight.T, block_out, preferred_element_type=jnp.float32).reshape(
        channels, lat_rows, lon_cols
    )


def add_terms(earlier, later):
    return earlier + later


def earlier_sum(increment):
    return entering(increment, "tm", add_terms, jnp.zeros_like(increment))


def shards(
    traj,
    noise,
    step_index,
    embed_weight,
    time_weight,
    dw_weight,
    ln_gain,
    up_weight,
    down_weight,
    out_weight,
):
    noise_level = noise_levels(step_index)
    condition = conditions(noise_level, time_weight)[0]
    level_now = noise_level[0]
    root = traj[0]
    anchor = spread(root, "tm", 0)
    current = root
    for picard_step in range(ITERS):
        drift_term = denoise(
            current, condition, embed_weight, dw_weight, ln_gain, up_weight, down_weight, out_weight
        )
        increment = 0.125 * level_now * drift_term + 0.125 * jnp.sqrt(level_now) * noise[0]
        current = anchor + earlier_sum(increment)
    return current[None]


def solution(mesh):
    in_specs = (
        P("tm", None, "lat", None),
        P("tm", None, "lat", None),
        P("tm"),
        P(),
        P(),
        P(),
        P(),
        P(),
        P(),
        P(),
    )
    out_specs = P("tm", None, "lat", None)
    return jax.shard_map(shards, mesh=mesh, in_specs=in_specs, out_specs=out_specs, check_vma=False)
```

profile of v0, /device:TPU:29, one launch (start us, length us, event | category | flops | bytes accessed | tf_op | source)
XLA Modules:
  0.0 318.5 jit_solution(5527043713613700483)
XLA Ops:
  7.4 1.8 fusion.162
  9.3 2.4 convert_reduce_fusion
  12.0 0.5 fusion.22
  12.6 0.6 copy.24
  13.3 3.7 %collective-permute-start = (bf16[512,2,192]{0,2,1:T(8,128)(2,1)S(1)}, bf16[512,2,192]{0,2,1:T(8,128)(2,1)S(1)}, u32[]{:S(2)}, u32[]{:S(2)}) collective-permute-start(bf16[512,2,192]{0,2,1:T(8,128)(2,1)S(1)} %get-tuple-element.87), channel_id=1, source_target_pairs={{0,1},{1,2},{2,3},{4,5},{5,6},{6,7},{8,9},{9,10},{10,11},{12,13},{... | collective-permute-start | bytes 1179656 | tf_op jit(solution)/shard_map/ppermute | solution.py:18
  17.0 1.9 collective-permute-start.1
  18.9 0.9 fusion.177
  19.8 1.2 fusion.176
  21.7 4.4 %collective-permute-done.1 = bf16[512,2,192]{0,2,1:T(8,128)(2,1)S(1)} collective-permute-done((bf16[512,2,192]{0,2,1:T(8,128)(2,1)S(1)}, bf16[512,2,192]{0,2,1:T(8,128)(2,1)S(1)}, u32[]{:S(2)}, u32[]{:S(2)}) %collective-permute-start.1) | collective-permute-done | bytes 393248 | tf_op jit(solution)/shard_map/ppermute | solution.py:19
  26.6 8.8 %fusion.170 = (f32[6,192]{1,0:T(8,128)S(1)}, f32[512,6,192]{0,2,1:T(8,128)S(1)}) fusion(f32[512,10,2]{0,2,1:T(2,128)S(1)} %get-tuple-element.84, f32[512,10,192]{0,2,1:T(8,128)S(1)} %maximum_convert_fusion, f32[512]{0:T(512)S(1)} %bitcast.124, f32[512]{0:T(512)S(1)} %bitcast.126, f32[512]{0:T(512)S(1)} %bitcast.130, ...), kind=kLoop, calls=%fused_computation.285 | loop fusion | flops 41286528 | bytes 18225664 | tf_op jit(solution)/shard_map/reduce_sum | solution.py:79
  35.5 0.5 multiply_reduce_fusion.1
  36.1 1.1 fusion.155
  37.2 3.5 %fusion.9 = bf16[1024,1152]{0,1:T(8,128)(2,1)} fusion(bf16[512,1152]{0,1:T(8,128)(2,1)S(1)} %fusion.155, bf16[512,1024]{1,0:T(8,128)(2,1)S(1)} %copy-done), kind=kOutput, calls=%fused_computation.51 | convolution fusion | flops 1218576384 | bytes 4587520 | tf_op jit(solution)/shard_map/dot_general | solution.py:86
  40.8 4.5 %fusion.24 = f32[83,1152]{1,0:T(8,128)} fusion(bf16[512,83]{0,1:T(8,128)(2,1)S(1)} %copy-done.47, bf16[1024,1152]{0,1:T(8,128)(2,1)} %fusion.9, bf16[1024,512]{1,0:T(8,128)(2,1)} %param.22, bf16[512,1152]{1,0:T(8,128)(2,1)S(1)} %copy-done.4, f32[]{:T(128)} %bitcast.3), kind=kOutput, calls=%fused_computation.108 | convolution fusion | flops 1307735424 | bytes 5054980 | tf_op jit(solution)/shard_map/dot_general | solution.py:92
  45.3 1.3 mul.669
  46.7 1.0 copy.27
  47.8 0.9 fusion.161
  48.7 70.6 %all-gather.3.cloned.1.call-done = f32[8,83,6,192]{3,1,2,0:T(8,128)} async-done(((f32[1,83,6,192]{3,1,2,0:T(8,128)}), f32[8,83,6,192]{3,1,2,0:T(8,128)}) %all-gather.3.cloned.1.call-update) | async-done | bytes 3059728 | tf_op jit(solution)/shard_map/all_gather | solution.py:26
  119.4 9.9 %while.20 = (s32[]{:T(128)}, f32[83,6,192]{2,1,0:T(8,128)S(1)}, s32[]{:T(128)}, f32[8,83,6,192]{3,1,2,0:T(8,128)}, s32[]{:T(128)}, /*index=5*/s32[]{:T(128)}, s32[]{:T(128)}) while((s32[]{:T(128)}, f32[83,6,192]{2,1,0:T(8,128)S(1)}, s32[]{:T(128)}, f32[8,83,6,192]{3,1,2,0:T(8,128)}, s32[]{:T(128)}, /*index=5*/s32[]{:T(128)}, s32[]{:T(128)}) %tuple.63), condition=%wide.region_4.5_spmd, body=%wide.region_3.4_spmd.sunk | while | flops 95621 | bytes 1912435 | solution.py:32
  119.4 1.1 constant_dynamic-slice_fusion.4
  120.8 1.1 constant_dynamic-slice_fusion.4
  122.2 1.1 constant_dynamic-slice_fusion.4
  123.6 1.1 constant_dynamic-slice_fusion.4
  125.0 1.1 constant_dynamic-slice_fusion.4
  126.4 1.1 constant_dynamic-slice_fusion.4
  127.8 1.1 constant_dynamic-slice_fusion.4
  129.4 63.4 %all-reduce.2.cloned.1.call-done = f32[83,6,192]{2,0,1:T(8,128)} async-done(((f32[83,6,192]{2,0,1:T(8,128)}), f32[83,6,192]{2,0,1:T(8,128)}) %all-reduce.2.cloned.1.call-update) | async-done | bytes 382480 | tf_op jit(solution)/shard_map/psum | solution.py:37
  192.7 1.2 fusion.160
  194.3 0.5 fusion.23
  194.9 5.7 %collective-permute-start.2 = (bf16[512,2,192]{0,2,1:T(8,128)(2,1)S(1)}, bf16[512,2,192]{0,2,1:T(8,128)(2,1)S(1)}, u32[]{:S(2)}, u32[]{:S(2)}) collective-permute-start(bf16[512,2,192]{0,2,1:T(8,128)(2,1)S(1)} %get-tuple-element.85), channel_id=1, source_target_pairs={{0,1},{1,2},{2,3},{4,5},{5,6},{6,7},{8,9},{9,10},{10,11},{12,13},{... | collective-permute-start | bytes 1179656 | tf_op jit(solution)/shard_map/ppermute | solution.py:18
  200.7 1.9 collective-permute-start.3
  202.6 2.6 collective-permute-done.2
  205.2 4.6 %collective-permute-done.3 = bf16[512,2,192]{0,2,1:T(8,128)(2,1)S(1)} collective-permute-done((bf16[512,2,192]{0,2,1:T(8,128)(2,1)S(1)}, bf16[512,2,192]{0,2,1:T(8,128)(2,1)S(1)}, u32[]{:S(2)}, u32[]{:S(2)}) %collective-permute-start.3) | collective-permute-done | bytes 393248 | tf_op jit(solution)/shard_map/ppermute | solution.py:19
  210.3 8.8 %fusion.168 = (f32[6,192]{1,0:T(8,128)S(1)}, f32[512,6,192]{0,2,1:T(8,128)S(1)}) fusion(f32[512,10,2]{0,2,1:T(2,128)S(1)} %get-tuple-element.82, f32[512,10,192]{0,2,1:T(8,128)S(1)} %maximum_convert_fusion.1, f32[512]{0:T(512)S(1)} %bitcast.125, f32[512]{0:T(512)S(1)} %bitcast.127, f32[512]{0:T(512)S(1)} %bitcast.131, ...), kind=kLoop, calls=%fused_computation.284 | loop fusion | flops 41286528 | bytes 18225664 | tf_op jit(solution)/shard_map/reduce_sum | solution.py:79
  219.3 0.5 multiply_reduce_fusion
  220.3 3.5 %fusion.17 = bf16[1024,1152]{0,1:T(8,128)(2,1)} fusion(bf16[512,1152]{0,1:T(8,128)(2,1)S(1)} %fusion.152, bf16[512,1024]{1,0:T(8,128)(2,1)S(1)} %copy-done), kind=kOutput, calls=%fused_computation.59 | convolution fusion | flops 1218576384 | bytes 4587520 | tf_op jit(solution)/shard_map/dot_general | solution.py:86
  223.9 3.7 %fusion.25 = f32[83,1152]{1,0:T(8,128)S(1)} fusion(bf16[512,83]{0,1:T(8,128)(2,1)S(1)} %copy-done.48, bf16[1024,1152]{0,1:T(8,128)(2,1)} %fusion.17, bf16[1024,512]{1,0:T(8,128)(2,1)} %param.22, bf16[1152,512]{1,0:T(8,128)(2,1)S(1)} %copy-done.2, f32[]{:T(128)} %bitcast.3), kind=kOutput, calls=%fused_computation.109 | convolution fusion | flops 1307735424 | bytes 5054980 | tf_op jit(solution)/shard_map/dot_general | solution.py:92
  228.0 1.0 copy.31
  229.0 71.6 %all-gather.5.cloned.1.call-done = f32[8,83,6,192]{3,1,2,0:T(8,128)} async-done(((f32[1,83,6,192]{3,1,2,0:T(8,128)}), f32[8,83,6,192]{3,1,2,0:T(8,128)}) %all-gather.5.cloned.1.call-update) | async-done | bytes 3059728 | tf_op jit(solution)/shard_map/all_gather | solution.py:26
  300.7 9.8 %while.21 = (s32[]{:T(128)}, f32[83,6,192]{2,1,0:T(8,128)S(1)}, s32[]{:T(128)}, f32[8,83,6,192]{3,1,2,0:T(8,128)}, s32[]{:T(128)}, /*index=5*/s32[]{:T(128)}, s32[]{:T(128)}) while((s32[]{:T(128)}, f32[83,6,192]{2,1,0:T(8,128)S(1)}, s32[]{:T(128)}, f32[8,83,6,192]{3,1,2,0:T(8,128)}, s32[]{:T(128)}, /*index=5*/s32[]{:T(128)}, s32[]{:T(128)}) %tuple.66), condition=%wide.region_8.9_spmd, body=%wide.region_7.8_spmd.sunk | while | flops 95621 | bytes 1912435 | solution.py:32
  300.7 1.1 constant_dynamic-slice_fusion.5
  302.1 1.1 constant_dynamic-slice_fusion.5
  303.5 1.1 constant_dynamic-slice_fusion.5
  304.9 1.1 constant_dynamic-slice_fusion.5
  306.3 1.1 constant_dynamic-slice_fusion.5
  307.7 1.1 constant_dynamic-slice_fusion.5
  309.1 1.1 constant_dynamic-slice_fusion.5
  310.7 1.3 copy.34
  (145 shorter events, 7.5 us)
Async XLA Ops:
  6.5 30.7 %copy-start = (bf16[512,1024]{1,0:T(8,128)(2,1)S(1)}, bf16[512,1024]{1,0:T(8,128)(2,1)}, u32[]{:S(2)}) copy-start(bf16[512,1024]{1,0:T(8,128)(2,1)} %param.21) | copy-start | bytes 3145732
  6.5 5.5 %copy-start.9 = (bf16[83,512]{1,0:T(8,128)(2,1)S(1)}, bf16[83,512]{1,0:T(8,128)(2,1)}, u32[]{:S(2)}) copy-start(bf16[83,512]{1,0:T(8,128)(2,1)} %param.17) | copy-start | bytes 254980
  6.5 112.8 %all-gather.3.cloned.1.call-start = ((), (), s32[]{:S(2)}) async-start(), calls=%async_computation.1 | async-start | bytes 4866048 | tf_op jit(solution)/shard_map/all_gather | solution.py:26
  12.6 13.8 %copy-start.3 = (bf16[512,1152]{1,0:T(8,128)(2,1)}, bf16[512,1152]{1,0:T(8,128)(2,1)S(1)}, u32[]{:S(2)}) copy-start(bf16[512,1152]{1,0:T(8,128)(2,1)S(1)} %fusion.22) | copy-start | bytes 3538948
  13.3 8.4 %collective-permute-start = (bf16[512,2,192]{0,2,1:T(8,128)(2,1)S(1)}, bf16[512,2,192]{0,2,1:T(8,128)(2,1)S(1)}, u32[]{:S(2)}, u32[]{:S(2)}) collective-permute-start(bf16[512,2,192]{0,2,1:T(8,128)(2,1)S(1)} %get-tuple-element.87), channel_id=1, source_target_pairs={{0,1},{1,2},{2,3},{4,5},{5,6},{6,7},{8,9},{9,10},{10,11},{12,13},{... | collective-permute-start | bytes 1179656 | tf_op jit(solution)/shard_map/ppermute | solution.py:18
  17.0 9.1 %collective-permute-start.1 = (bf16[512,2,192]{0,2,1:T(8,128)(2,1)S(1)}, bf16[512,2,192]{0,2,1:T(8,128)(2,1)S(1)}, u32[]{:S(2)}, u32[]{:S(2)}) collective-permute-start(bf16[512,2,192]{0,2,1:T(8,128)(2,1)S(1)} %get-tuple-element.88), channel_id=1, source_target_pairs={{1,0},{2,1},{3,2},{5,4},{6,5},{7,6},{9,8},{10,9},{11,10},{13,12},{... | collective-permute-start | bytes 1179656 | tf_op jit(solution)/shard_map/ppermute | solution.py:19
  21.0 5.3 %copy-start.10 = (f32[512,1]{0,1:T(1,128)}, f32[512,1]{0,1:T(1,128)S(1)}, u32[]{:S(2)}) copy-start(f32[512,1]{0,1:T(1,128)S(1)} %get-tuple-element.91) | copy-start | bytes 6148
  21.1 5.3 %copy-start.12 = (f32[512,1]{0,1:T(1,128)}, f32[512,1]{0,1:T(1,128)S(1)}, u32[]{:S(2)}) copy-start(f32[512,1]{0,1:T(1,128)S(1)} %get-tuple-element.92) | copy-start | bytes 6148
  21.1 5.3 %copy-start.14 = (f32[512,1]{0,1:T(1,128)}, f32[512,1]{0,1:T(1,128)S(1)}, u32[]{:S(2)}) copy-start(f32[512,1]{0,1:T(1,128)S(1)} %get-tuple-element.93) | copy-start | bytes 6148
  21.1 5.3 %copy-start.16 = (f32[512,1]{0,1:T(1,128)}, f32[512,1]{0,1:T(1,128)S(1)}, u32[]{:S(2)}) copy-start(f32[512,1]{0,1:T(1,128)S(1)} %get-tuple-element.94) | copy-start | bytes 6148
  21.1 5.3 %copy-start.18 = (f32[512,1]{0,1:T(1,128)}, f32[512,1]{0,1:T(1,128)S(1)}, u32[]{:S(2)}) copy-start(f32[512,1]{0,1:T(1,128)S(1)} %get-tuple-element.95) | copy-start | bytes 6148
  21.1 5.3 %copy-start.20 = (f32[512,1]{0,1:T(1,128)}, f32[512,1]{0,1:T(1,128)S(1)}, u32[]{:S(2)}) copy-start(f32[512,1]{0,1:T(1,128)S(1)} %get-tuple-element.96) | copy-start | bytes 6148
  21.1 5.3 %copy-start.22 = (f32[512,1]{0,1:T(1,128)}, f32[512,1]{0,1:T(1,128)S(1)}, u32[]{:S(2)}) copy-start(f32[512,1]{0,1:T(1,128)S(1)} %get-tuple-element.97) | copy-start | bytes 6148
  21.1 5.3 %copy-start.24 = (f32[512,1]{0,1:T(1,128)}, f32[512,1]{0,1:T(1,128)S(1)}, u32[]{:S(2)}) copy-start(f32[512,1]{0,1:T(1,128)S(1)} %get-tuple-element.98) | copy-start | bytes 6148
  21.1 5.3 %copy-start.26 = (f32[512,1]{0,1:T(1,128)}, f32[512,1]{0,1:T(1,128)S(1)}, u32[]{:S(2)}) copy-start(f32[512,1]{0,1:T(1,128)S(1)} %get-tuple-element.99) | copy-start | bytes 6148
  21.1 5.3 %copy-start.28 = (f32[512,1]{0,1:T(1,128)}, f32[512,1]{0,1:T(1,128)S(1)}, u32[]{:S(2)}) copy-start(f32[512,1]{0,1:T(1,128)S(1)} %get-tuple-element.100) | copy-start | bytes 6148
  21.1 5.3 %copy-start.30 = (f32[512,1]{0,1:T(1,128)}, f32[512,1]{0,1:T(1,128)S(1)}, u32[]{:S(2)}) copy-start(f32[512,1]{0,1:T(1,128)S(1)} %get-tuple-element.101) | copy-start | bytes 6148
  21.2 5.3 %copy-start.32 = (f32[512,1]{0,1:T(1,128)}, f32[512,1]{0,1:T(1,128)S(1)}, u32[]{:S(2)}) copy-start(f32[512,1]{0,1:T(1,128)S(1)} %get-tuple-element.102) | copy-start | bytes 6148
  21.2 5.3 %copy-start.34 = (f32[512,1]{0,1:T(1,128)}, f32[512,1]{0,1:T(1,128)S(1)}, u32[]{:S(2)}) copy-start(f32[512,1]{0,1:T(1,128)S(1)} %get-tuple-element.103) | copy-start | bytes 6148
  21.2 5.3 %copy-start.36 = (f32[512,1]{0,1:T(1,128)}, f32[512,1]{0,1:T(1,128)S(1)}, u32[]{:S(2)}) copy-start(f32[512,1]{0,1:T(1,128)S(1)} %get-tuple-element.104) | copy-start | bytes 6148
  21.2 5.3 %copy-start.38 = (f32[512,1]{0,1:T(1,128)}, f32[512,1]{0,1:T(1,128)S(1)}, u32[]{:S(2)}) copy-start(f32[512,1]{0,1:T(1,128)S(1)} %get-tuple-element.105) | copy-start | bytes 6148
  21.2 5.3 %copy-start.40 = (f32[512,1]{0,1:T(1,128)}, f32[512,1]{0,1:T(1,128)S(1)}, u32[]{:S(2)}) copy-start(f32[512,1]{0,1:T(1,128)S(1)} %get-tuple-element.106) | copy-start | bytes 6148
  21.2 5.3 %copy-start.42 = (f32[512,1]{0,1:T(1,128)}, f32[512,1]{0,1:T(1,128)S(1)}, u32[]{:S(2)}) copy-start(f32[512,1]{0,1:T(1,128)S(1)} %get-tuple-element.107) | copy-start | bytes 6148
  40.8 5.8 %copy-start.6 = (f32[1,83,6,192]{3,0,2,1:T(1,128)S(1)}, f32[1,83,6,192]{3,0,2,1:T(1,128)}, u32[]{:S(2)}) copy-start(f32[1,83,6,192]{3,0,2,1:T(1,128)} %param.15) | copy-start | bytes 1147396
  47.7 145.0 %all-reduce.2.cloned.1.call-start = ((), (), s32[]{:S(2)}) async-start(), calls=%async_computation | async-start | bytes 1081344 | tf_op jit(solution)/shard_map/psum | solution.py:37
  48.7 251.9 %all-gather.5.cloned.1.call-start = ((), (), s32[]{:S(2)}) async-start(), calls=%async_computation.2 | async-start | bytes 4866048 | tf_op jit(solution)/shard_map/all_gather | solution.py:26
  129.3 65.0 %copy-start.45 = (f32[512]{0:T(512)S(1)}, f32[512]{0:T(512)}, u32[]{:S(2)}) copy-start(f32[512]{0:T(512)} %copy-done.44) | copy-start | bytes 6148
  194.8 15.3 %copy-start.1 = (bf16[1152,512]{1,0:T(8,128)(2,1)}, bf16[1152,512]{1,0:T(8,128)(2,1)S(1)}, u32[]{:S(2)}) copy-start(bf16[1152,512]{1,0:T(8,128)(2,1)S(1)} %fusion.23) | copy-start | bytes 3538948
  194.9 10.4 %collective-permute-start.2 = (bf16[512,2,192]{0,2,1:T(8,128)(2,1)S(1)}, bf16[512,2,192]{0,2,1:T(8,128)(2,1)S(1)}, u32[]{:S(2)}, u32[]{:S(2)}) collective-permute-start(bf16[512,2,192]{0,2,1:T(8,128)(2,1)S(1)} %get-tuple-element.85), channel_id=1, source_target_pairs={{0,1},{1,2},{2,3},{4,5},{5,6},{6,7},{8,9},{9,10},{10,11},{12,13},{... | collective-permute-start | bytes 1179656 | tf_op jit(solution)/shard_map/ppermute | solution.py:18
  200.5 9.6 %copy-start.11 = (f32[512,1]{0,1:T(1,128)S(1)}, f32[512,1]{0,1:T(1,128)}, u32[]{:S(2)}) copy-start(f32[512,1]{0,1:T(1,128)} %copy-done.10) | copy-start | bytes 6148
  200.6 9.6 %copy-start.13 = (f32[512,1]{0,1:T(1,128)S(1)}, f32[512,1]{0,1:T(1,128)}, u32[]{:S(2)}) copy-start(f32[512,1]{0,1:T(1,128)} %copy-done.12) | copy-start | bytes 6148
  200.6 9.6 %copy-start.15 = (f32[512,1]{0,1:T(1,128)S(1)}, f32[512,1]{0,1:T(1,128)}, u32[]{:S(2)}) copy-start(f32[512,1]{0,1:T(1,128)} %copy-done.14) | copy-start | bytes 6148
  200.6 9.6 %copy-start.17 = (f32[512,1]{0,1:T(1,128)S(1)}, f32[512,1]{0,1:T(1,128)}, u32[]{:S(2)}) copy-start(f32[512,1]{0,1:T(1,128)} %copy-done.16) | copy-start | bytes 6148
  200.6 9.6 %copy-start.19 = (f32[512,1]{0,1:T(1,128)S(1)}, f32[512,1]{0,1:T(1,128)}, u32[]{:S(2)}) copy-start(f32[512,1]{0,1:T(1,128)} %copy-done.18) | copy-start | bytes 6148
  200.6 9.6 %copy-start.21 = (f32[512,1]{0,1:T(1,128)S(1)}, f32[512,1]{0,1:T(1,128)}, u32[]{:S(2)}) copy-start(f32[512,1]{0,1:T(1,128)} %copy-done.20) | copy-start | bytes 6148
  200.6 9.6 %copy-start.23 = (f32[512,1]{0,1:T(1,128)S(1)}, f32[512,1]{0,1:T(1,128)}, u32[]{:S(2)}) copy-start(f32[512,1]{0,1:T(1,128)} %copy-done.22) | copy-start | bytes 6148
  200.6 9.6 %copy-start.25 = (f32[512,1]{0,1:T(1,128)S(1)}, f32[512,1]{0,1:T(1,128)}, u32[]{:S(2)}) copy-start(f32[512,1]{0,1:T(1,128)} %copy-done.24) | copy-start | bytes 6148
  200.6 9.6 %copy-start.27 = (f32[512,1]{0,1:T(1,128)S(1)}, f32[512,1]{0,1:T(1,128)}, u32[]{:S(2)}) copy-start(f32[512,1]{0,1:T(1,128)} %copy-done.26) | copy-start | bytes 6148
  200.6 9.6 %copy-start.29 = (f32[512,1]{0,1:T(1,128)S(1)}, f32[512,1]{0,1:T(1,128)}, u32[]{:S(2)}) copy-start(f32[512,1]{0,1:T(1,128)} %copy-done.28) | copy-start | bytes 6148
  200.6 9.6 %copy-start.31 = (f32[512,1]{0,1:T(1,128)S(1)}, f32[512,1]{0,1:T(1,128)}, u32[]{:S(2)}) copy-start(f32[512,1]{0,1:T(1,128)} %copy-done.30) | copy-start | bytes 6148
  200.7 9.6 %copy-start.33 = (f32[512,1]{0,1:T(1,128)S(1)}, f32[512,1]{0,1:T(1,128)}, u32[]{:S(2)}) copy-start(f32[512,1]{0,1:T(1,128)} %copy-done.32) | copy-start | bytes 6148
  200.7 9.6 %copy-start.35 = (f32[512,1]{0,1:T(1,128)S(1)}, f32[512,1]{0,1:T(1,128)}, u32[]{:S(2)}) copy-start(f32[512,1]{0,1:T(1,128)} %copy-done.34) | copy-start | bytes 6148
  200.7 9.6 %copy-start.37 = (f32[512,1]{0,1:T(1,128)S(1)}, f32[512,1]{0,1:T(1,128)}, u32[]{:S(2)}) copy-start(f32[512,1]{0,1:T(1,128)} %copy-done.36) | copy-start | bytes 6148
  200.7 9.6 %copy-start.39 = (f32[512,1]{0,1:T(1,128)S(1)}, f32[512,1]{0,1:T(1,128)}, u32[]{:S(2)}) copy-start(f32[512,1]{0,1:T(1,128)} %copy-done.38) | copy-start | bytes 6148
  200.7 9.6 %copy-start.41 = (f32[512,1]{0,1:T(1,128)S(1)}, f32[512,1]{0,1:T(1,128)}, u32[]{:S(2)}) copy-start(f32[512,1]{0,1:T(1,128)} %copy-done.40) | copy-start | bytes 6148
  200.7 9.6 %copy-start.43 = (f32[512,1]{0,1:T(1,128)S(1)}, f32[512,1]{0,1:T(1,128)}, u32[]{:S(2)}) copy-start(f32[512,1]{0,1:T(1,128)} %copy-done.42) | copy-start | bytes 6148
  200.7 9.1 %collective-permute-start.3 = (bf16[512,2,192]{0,2,1:T(8,128)(2,1)S(1)}, bf16[512,2,192]{0,2,1:T(8,128)(2,1)S(1)}, u32[]{:S(2)}, u32[]{:S(2)}) collective-permute-start(bf16[512,2,192]{0,2,1:T(8,128)(2,1)S(1)} %get-tuple-element.86), channel_id=1, source_target_pairs={{1,0},{2,1},{3,2},{5,4},{6,5},{7,6},{9,8},{10,9},{11,10},{13,12},{... | collective-permute-start | bytes 1179656 | tf_op jit(solution)/shard_map/ppermute | solution.py:19
  300.6 9.8 %copy-start.5 = (f32[83,6,192]{2,0,1:T(8,128)S(1)}, f32[83,6,192]{2,0,1:T(8,128)}, u32[]{:S(2)}) copy-start(f32[83,6,192]{2,0,1:T(8,128)} %all-reduce.2.cloned.1.call-done) | copy-start | bytes 1147396
  (8 other events, 24.2 us)
Sparse Core Ops, SparseCore 0:
  47.8 71.4 all-gather.2
  122.7 69.9 all-reduce.1
  229.1 71.4 all-gather.4
where the time goes:
time: 320 us; the launch traced here: 319 us
  waiting for transfers between devices  218 us (68%)
  other arithmetic  29.6 us (9%)
  local copies, waits for them, and re-layouts  24.2 us (8%)
  matrix products  18.1 us (6%)
  between operations  14.9 us (5%)
  starting transfers between devices  13.3 us (4%)
    all_gather x2, waiting for transfers between devices, entering(): gathered = lax.all_gather(part, axis)  142 us
    psum x1, waiting for transfers between devices, spread(): return lax.psum(kept, axis)  63.4 us
    reduce_sum x2, other arithmetic, denoise(): average = jnp.mean(convolved, axis=0)  17.7 us
    dynamic_slice x14, local copies, waits for them, and re-layouts, one(): return combine(state, lax.dynamic_index_in_dim(gathered, turn, 0, False))  15.3 us
    ppermute x2, starting transfers between devices, with_halo(): before = lax.ppermute(last, axis, up)  9.34 us
    ppermute x2, waiting for transfers between devices, with_halo(): after = lax.ppermute(first, axis, down)  8.96 us
    dot_general x2, matrix products, denoise(): jnp.dot(out_weight.T, block_out, preferred_element_type=jnp.float32)  8.2 us
    dot_general x2, matrix products, denoise(): jnp.dot(up_weight.T, normed, preferred_element_type=jnp.float32)  7.08 us
  transfers between devices with their start and end apart: 7, of which 7 were waited for; matrix products, arithmetic and copies ran while one was open for 4% of the time, Pallas kernels for 0%

commit v1 on v0

--- a/solution.py
+++ b/solution.py
@@ -34,7 +34,7 @@
 
 def spread(value, axis, source):
     kept = jnp.where(lax.axis_index(axis) == source, value, 0).astype(value.dtype)
-    return lax.psum(kept, axis)
+    return jnp.sum(lax.all_gather(kept, axis), axis=0)
 
 
 def noise_levels(step_index):

time: 320 us -> 291 us (0.909)
  waiting for transfers between devices: 218 us -> 192 us
    psum x1 -> x0, waiting for transfers between devices: 63.4 us -> none  [spread(): return lax.psum(kept, axis)]
    all_gather x0 -> x1, waiting for transfers between devices: none -> 34.9 us  [spread(): return jnp.sum(lax.all_gather(kept, axis), axis=0)]
  transfers between devices with their start and end apart: 7 -> 7, of which waited for: 7 -> 7; matrix products, arithmetic and copies ran while one was open for 4% -> 10% of each run, Pallas kernels for 0% -> 0%
where the time goes in v1:
time: 291 us; the launch traced here: 290 us
  waiting for transfers between devices  192 us (66%)
  other arithmetic  32.4 us (11%)
  local copies, waits for them, and re-layouts  23.3 us (8%)
  matrix products  16.2 us (6%)
  between operations  14.8 us (5%)
  starting transfers between devices  11.3 us (4%)
    all_gather x2, waiting for transfers between devices, entering(): gathered = lax.all_gather(part, axis)  144 us
    all_gather x1, waiting for transfers between devices, spread(): return jnp.sum(lax.all_gather(kept, axis), axis=0)  34.9 us
    reduce_sum x2, other arithmetic, denoise(): average = jnp.mean(convolved, axis=0)  17.7 us
    dynamic_slice x14, local copies, waits for them, and re-layouts, one(): return combine(state, lax.dynamic_index_in_dim(gathered, turn, 0, False))  15.3 us
    ppermute x2, waiting for transfers between devices, with_halo(): after = lax.ppermute(first, axis, down)  9.36 us
    dot_general x2, matrix products, denoise(): jnp.dot(out_weight.T, block_out, preferred_element_type=jnp.float32)  7.49 us
    ppermute x2, starting transfers between devices, with_halo(): before = lax.ppermute(last, axis, up)  7.34 us
    dot_general x2, matrix products, denoise(): jnp.dot(up_weight.T, normed, preferred_element_type=jnp.float32)  7.1 us
  transfers between devices with their start and end apart: 7, of which 7 were waited for; matrix products, arithmetic and copies ran while one was open for 10% of the time, Pallas kernels for 0%

profile of v1, /device:TPU:29, one launch (start us, length us, event | category | flops | bytes accessed | tf_op | source)
XLA Modules:
  0.0 290.3 jit_solution(9757228013607176005)
XLA Ops:
  6.6 2.0 copy_select_fusion
  8.7 2.4 convert_reduce_fusion
  11.9 0.6 fusion.161
  13.1 0.5 fusion.22
  13.7 0.6 copy.23
  14.3 3.7 %collective-permute-start = (bf16[512,2,192]{0,2,1:T(8,128)(2,1)S(1)}, bf16[512,2,192]{0,2,1:T(8,128)(2,1)S(1)}, u32[]{:S(2)}, u32[]{:S(2)}) collective-permute-start(bf16[512,2,192]{0,2,1:T(8,128)(2,1)S(1)} %get-tuple-element.87), channel_id=1, source_target_pairs={{0,1},{1,2},{2,3},{4,5},{5,6},{6,7},{8,9},{9,10},{10,11},{12,13},{... | collective-permute-start | bytes 1179656 | tf_op jit(solution)/shard_map/ppermute | solution.py:18
  18.0 1.9 collective-permute-start.1
  20.0 0.9 fusion.176
  20.9 1.2 fusion.175
  22.2 0.5 collective-permute-done
  22.7 4.8 %collective-permute-done.1 = bf16[512,2,192]{0,2,1:T(8,128)(2,1)S(1)} collective-permute-done((bf16[512,2,192]{0,2,1:T(8,128)(2,1)S(1)}, bf16[512,2,192]{0,2,1:T(8,128)(2,1)S(1)}, u32[]{:S(2)}, u32[]{:S(2)}) %collective-permute-start.1) | collective-permute-done | bytes 393248 | tf_op jit(solution)/shard_map/ppermute | solution.py:19
  28.1 8.8 %fusion.169 = (f32[6,192]{1,0:T(8,128)S(1)}, f32[512,6,192]{0,2,1:T(8,128)S(1)}) fusion(f32[512,10,2]{0,2,1:T(2,128)S(1)} %get-tuple-element.84, f32[512,10,192]{0,2,1:T(8,128)S(1)} %maximum_convert_fusion, f32[512]{0:T(512)S(1)} %bitcast.122, f32[512]{0:T(512)S(1)} %bitcast.124, f32[512]{0:T(512)S(1)} %bitcast.128, ...), kind=kLoop, calls=%fused_computation.284 | loop fusion | flops 41286528 | bytes 18225664 | tf_op jit(solution)/shard_map/reduce_sum | solution.py:79
  37.0 0.5 multiply_reduce_fusion.1
  37.6 1.1 fusion.155
  38.7 3.6 %fusion.9 = bf16[1024,1152]{0,1:T(8,128)(2,1)} fusion(bf16[512,1152]{0,1:T(8,128)(2,1)S(1)} %fusion.155, bf16[512,1024]{1,0:T(8,128)(2,1)S(1)} %copy-done), kind=kOutput, calls=%fused_computation.51 | convolution fusion | flops 1218576384 | bytes 4587520 | tf_op jit(solution)/shard_map/dot_general | solution.py:86
  42.3 3.8 %fusion.24 = f32[83,1152]{1,0:T(8,128)S(1)} fusion(bf16[512,83]{0,1:T(8,128)(2,1)S(1)} %copy-done.48, bf16[1024,1152]{0,1:T(8,128)(2,1)} %fusion.9, bf16[1024,512]{1,0:T(8,128)(2,1)} %param.22, bf16[512,1152]{1,0:T(8,128)(2,1)S(1)} %copy-done.6, f32[]{:T(128)} %bitcast.2), kind=kOutput, calls=%fused_computation.108 | convolution fusion | flops 1307735424 | bytes 5054980 | tf_op jit(solution)/shard_map/dot_general | solution.py:92
  46.5 1.0 copy.26
  47.5 34.9 %all-gather.4.cloned.1.call-done = f32[8,83,6,192]{3,1,2,0:T(8,128)} async-done(((f32[1,83,6,192]{3,1,2,0:T(8,128)}), f32[8,83,6,192]{3,1,2,0:T(8,128)}) %all-gather.4.cloned.1.call-update) | async-done | bytes 3059728 | tf_op jit(solution)/shard_map/all_gather | solution.py:37
  82.5 2.6 reduce_sum.45
  85.1 72.5 %all-gather.6.cloned.1.call-done = f32[8,83,6,192]{3,1,2,0:T(8,128)} async-done(((f32[1,83,6,192]{3,1,2,0:T(8,128)}), f32[8,83,6,192]{3,1,2,0:T(8,128)}) %all-gather.6.cloned.1.call-update) | async-done | bytes 3059728 | tf_op jit(solution)/shard_map/all_gather | solution.py:26
  157.6 9.9 %while.20 = (s32[]{:T(128)}, f32[83,6,192]{2,1,0:T(8,128)S(1)}, s32[]{:T(128)}, f32[8,83,6,192]{3,1,2,0:T(8,128)}, s32[]{:T(128)}, /*index=5*/s32[]{:T(128)}, s32[]{:T(128)}) while((s32[]{:T(128)}, f32[83,6,192]{2,1,0:T(8,128)S(1)}, s32[]{:T(128)}, f32[8,83,6,192]{3,1,2,0:T(8,128)}, s32[]{:T(128)}, /*index=5*/s32[]{:T(128)}, s32[]{:T(128)}) %tuple.63), condition=%wide.region_4.5_spmd, body=%wide.region_3.4_spmd.sunk | while | flops 95621 | bytes 1912435 | solution.py:32
  157.7 1.1 constant_dynamic-slice_fusion.4
  159.1 1.1 constant_dynamic-slice_fusion.4
  160.5 1.1 constant_dynamic-slice_fusion.4
  161.9 1.1 constant_dynamic-slice_fusion.4
  163.2 1.1 constant_dynamic-slice_fusion.4
  164.6 1.1 constant_dynamic-slice_fusion.4
  166.0 1.1 constant_dynamic-slice_fusion.4
  168.1 0.5 fusion.23
  168.7 3.7 %collective-permute-start.2 = (bf16[512,2,192]{0,2,1:T(8,128)(2,1)S(1)}, bf16[512,2,192]{0,2,1:T(8,128)(2,1)S(1)}, u32[]{:S(2)}, u32[]{:S(2)}) collective-permute-start(bf16[512,2,192]{0,2,1:T(8,128)(2,1)S(1)} %get-tuple-element.85), channel_id=1, source_target_pairs={{0,1},{1,2},{2,3},{4,5},{5,6},{6,7},{8,9},{9,10},{10,11},{12,13},{... | collective-permute-start | bytes 1179656 | tf_op jit(solution)/shard_map/ppermute | solution.py:18
  172.5 1.9 collective-permute-start.3
  174.5 2.6 collective-permute-done.2
  177.1 4.6 %collective-permute-done.3 = bf16[512,2,192]{0,2,1:T(8,128)(2,1)S(1)} collective-permute-done((bf16[512,2,192]{0,2,1:T(8,128)(2,1)S(1)}, bf16[512,2,192]{0,2,1:T(8,128)(2,1)S(1)}, u32[]{:S(2)}, u32[]{:S(2)}) %collective-permute-start.3) | collective-permute-done | bytes 393248 | tf_op jit(solution)/shard_map/ppermute | solution.py:19
  182.1 8.8 %fusion.167 = (f32[6,192]{1,0:T(8,128)S(1)}, f32[512,6,192]{0,2,1:T(8,128)S(1)}) fusion(f32[512,10,2]{0,2,1:T(2,128)S(1)} %get-tuple-element.82, f32[512,10,192]{0,2,1:T(8,128)S(1)} %maximum_convert_fusion.1, f32[512]{0:T(512)S(1)} %bitcast.123, f32[512]{0:T(512)S(1)} %bitcast.125, f32[512]{0:T(512)S(1)} %bitcast.129, ...), kind=kLoop, calls=%fused_computation.283 | loop fusion | flops 41286528 | bytes 18225664 | tf_op jit(solution)/shard_map/reduce_sum | solution.py:79
  191.1 0.5 multiply_reduce_fusion
  192.1 3.5 %fusion.17 = bf16[1024,1152]{0,1:T(8,128)(2,1)} fusion(bf16[512,1152]{0,1:T(8,128)(2,1)S(1)} %fusion.152, bf16[512,1024]{1,0:T(8,128)(2,1)S(1)} %copy-done), kind=kOutput, calls=%fused_computation.59 | convolution fusion | flops 1218576384 | bytes 4587520 | tf_op jit(solution)/shard_map/dot_general | solution.py:86
  195.6 3.7 %fusion.25 = f32[83,1152]{1,0:T(8,128)S(1)} fusion(bf16[512,83]{0,1:T(8,128)(2,1)S(1)} %copy-done.49, bf16[1024,1152]{0,1:T(8,128)(2,1)} %fusion.17, bf16[1024,512]{1,0:T(8,128)(2,1)} %param.22, bf16[1152,512]{1,0:T(8,128)(2,1)S(1)} %copy-done.2, f32[]{:T(128)} %bitcast.2), kind=kOutput, calls=%fused_computation.109 | convolution fusion | flops 1307735424 | bytes 5054980 | tf_op jit(solution)/shard_map/dot_general | solution.py:92
  199.8 1.0 copy.28
  200.8 71.6 %all-gather.8.cloned.1.call-done = f32[8,83,6,192]{3,1,2,0:T(8,128)} async-done(((f32[1,83,6,192]{3,1,2,0:T(8,128)}), f32[8,83,6,192]{3,1,2,0:T(8,128)}) %all-gather.8.cloned.1.call-update) | async-done | bytes 3059728 | tf_op jit(solution)/shard_map/all_gather | solution.py:26
  272.4 9.8 %while.21 = (s32[]{:T(128)}, f32[83,6,192]{2,1,0:T(8,128)S(1)}, s32[]{:T(128)}, f32[8,83,6,192]{3,1,2,0:T(8,128)}, s32[]{:T(128)}, /*index=5*/s32[]{:T(128)}, s32[]{:T(128)}) while((s32[]{:T(128)}, f32[83,6,192]{2,1,0:T(8,128)S(1)}, s32[]{:T(128)}, f32[8,83,6,192]{3,1,2,0:T(8,128)}, s32[]{:T(128)}, /*index=5*/s32[]{:T(128)}, s32[]{:T(128)}) %tuple.66), condition=%wide.region_8.9_spmd, body=%wide.region_7.8_spmd.sunk | while | flops 95621 | bytes 1912435 | solution.py:32
  272.5 1.1 constant_dynamic-slice_fusion.5
  273.9 1.1 constant_dynamic-slice_fusion.5
  275.3 1.1 constant_dynamic-slice_fusion.5
  276.7 1.1 constant_dynamic-slice_fusion.5
  278.1 1.1 constant_dynamic-slice_fusion.5
  279.5 1.1 constant_dynamic-slice_fusion.5
  280.9 1.1 constant_dynamic-slice_fusion.5
  282.5 1.3 copy.31
  (147 shorter events, 7.8 us)
Async XLA Ops:
  6.5 32.1 %copy-start = (bf16[512,1024]{1,0:T(8,128)(2,1)S(1)}, bf16[512,1024]{1,0:T(8,128)(2,1)}, u32[]{:S(2)}) copy-start(bf16[512,1024]{1,0:T(8,128)(2,1)} %param.21) | copy-start | bytes 3145732
  6.5 6.6 %copy-start.10 = (bf16[83,512]{1,0:T(8,128)(2,1)S(1)}, bf16[83,512]{1,0:T(8,128)(2,1)}, u32[]{:S(2)}) copy-start(bf16[83,512]{1,0:T(8,128)(2,1)} %param.17) | copy-start | bytes 254980
  6.5 75.9 %all-gather.4.cloned.1.call-start = ((), (), s32[]{:S(2)}) async-start(), calls=%async_computation | async-start | bytes 4866048 | tf_op jit(solution)/shard_map/all_gather | solution.py:37
  8.6 149.0 %all-gather.6.cloned.1.call-start = ((), (), s32[]{:S(2)}) async-start(), calls=%async_computation.1 | async-start | bytes 4866048 | tf_op jit(solution)/shard_map/all_gather | solution.py:26
  13.6 14.2 %copy-start.5 = (bf16[512,1152]{1,0:T(8,128)(2,1)}, bf16[512,1152]{1,0:T(8,128)(2,1)S(1)}, u32[]{:S(2)}) copy-start(bf16[512,1152]{1,0:T(8,128)(2,1)S(1)} %fusion.22) | copy-start | bytes 3538948
  14.3 8.4 %collective-permute-start = (bf16[512,2,192]{0,2,1:T(8,128)(2,1)S(1)}, bf16[512,2,192]{0,2,1:T(8,128)(2,1)S(1)}, u32[]{:S(2)}, u32[]{:S(2)}) collective-permute-start(bf16[512,2,192]{0,2,1:T(8,128)(2,1)S(1)} %get-tuple-element.87), channel_id=1, source_target_pairs={{0,1},{1,2},{2,3},{4,5},{5,6},{6,7},{8,9},{9,10},{10,11},{12,13},{... | collective-permute-start | bytes 1179656 | tf_op jit(solution)/shard_map/ppermute | solution.py:18
  18.0 9.5 %collective-permute-start.1 = (bf16[512,2,192]{0,2,1:T(8,128)(2,1)S(1)}, bf16[512,2,192]{0,2,1:T(8,128)(2,1)S(1)}, u32[]{:S(2)}, u32[]{:S(2)}) collective-permute-start(bf16[512,2,192]{0,2,1:T(8,128)(2,1)S(1)} %get-tuple-element.88), channel_id=1, source_target_pairs={{1,0},{2,1},{3,2},{5,4},{6,5},{7,6},{9,8},{10,9},{11,10},{13,12},{... | collective-permute-start | bytes 1179656 | tf_op jit(solution)/shard_map/ppermute | solution.py:19
  22.1 5.8 %copy-start.11 = (f32[512,1]{0,1:T(1,128)}, f32[512,1]{0,1:T(1,128)S(1)}, u32[]{:S(2)}) copy-start(f32[512,1]{0,1:T(1,128)S(1)} %get-tuple-element.91) | copy-start | bytes 6148
  22.1 5.8 %copy-start.13 = (f32[512,1]{0,1:T(1,128)}, f32[512,1]{0,1:T(1,128)S(1)}, u32[]{:S(2)}) copy-start(f32[512,1]{0,1:T(1,128)S(1)} %get-tuple-element.92) | copy-start | bytes 6148
  22.1 5.8 %copy-start.15 = (f32[512,1]{0,1:T(1,128)}, f32[512,1]{0,1:T(1,128)S(1)}, u32[]{:S(2)}) copy-start(f32[512,1]{0,1:T(1,128)S(1)} %get-tuple-element.93) | copy-start | bytes 6148
  22.1 5.8 %copy-start.17 = (f32[512,1]{0,1:T(1,128)}, f32[512,1]{0,1:T(1,128)S(1)}, u32[]{:S(2)}) copy-start(f32[512,1]{0,1:T(1,128)S(1)} %get-tuple-element.94) | copy-start | bytes 6148
  22.1 5.8 %copy-start.19 = (f32[512,1]{0,1:T(1,128)}, f32[512,1]{0,1:T(1,128)S(1)}, u32[]{:S(2)}) copy-start(f32[512,1]{0,1:T(1,128)S(1)} %get-tuple-element.95) | copy-start | bytes 6148
  22.1 5.8 %copy-start.21 = (f32[512,1]{0,1:T(1,128)}, f32[512,1]{0,1:T(1,128)S(1)}, u32[]{:S(2)}) copy-start(f32[512,1]{0,1:T(1,128)S(1)} %get-tuple-element.96) | copy-start | bytes 6148
  22.1 5.8 %copy-start.23 = (f32[512,1]{0,1:T(1,128)}, f32[512,1]{0,1:T(1,128)S(1)}, u32[]{:S(2)}) copy-start(f32[512,1]{0,1:T(1,128)S(1)} %get-tuple-element.97) | copy-start | bytes 6148
  22.1 5.8 %copy-start.25 = (f32[512,1]{0,1:T(1,128)}, f32[512,1]{0,1:T(1,128)S(1)}, u32[]{:S(2)}) copy-start(f32[512,1]{0,1:T(1,128)S(1)} %get-tuple-element.98) | copy-start | bytes 6148
  22.2 5.8 %copy-start.27 = (f32[512,1]{0,1:T(1,128)}, f32[512,1]{0,1:T(1,128)S(1)}, u32[]{:S(2)}) copy-start(f32[512,1]{0,1:T(1,128)S(1)} %get-tuple-element.99) | copy-start | bytes 6148
  22.2 5.8 %copy-start.29 = (f32[512,1]{0,1:T(1,128)}, f32[512,1]{0,1:T(1,128)S(1)}, u32[]{:S(2)}) copy-start(f32[512,1]{0,1:T(1,128)S(1)} %get-tuple-element.100) | copy-start | bytes 6148
  22.2 5.8 %copy-start.31 = (f32[512,1]{0,1:T(1,128)}, f32[512,1]{0,1:T(1,128)S(1)}, u32[]{:S(2)}) copy-start(f32[512,1]{0,1:T(1,128)S(1)} %get-tuple-element.101) | copy-start | bytes 6148
  22.2 5.8 %copy-start.33 = (f32[512,1]{0,1:T(1,128)}, f32[512,1]{0,1:T(1,128)S(1)}, u32[]{:S(2)}) copy-start(f32[512,1]{0,1:T(1,128)S(1)} %get-tuple-element.102) | copy-start | bytes 6148
  22.2 5.8 %copy-start.35 = (f32[512,1]{0,1:T(1,128)}, f32[512,1]{0,1:T(1,128)S(1)}, u32[]{:S(2)}) copy-start(f32[512,1]{0,1:T(1,128)S(1)} %get-tuple-element.103) | copy-start | bytes 6148
  22.2 5.8 %copy-start.37 = (f32[512,1]{0,1:T(1,128)}, f32[512,1]{0,1:T(1,128)S(1)}, u32[]{:S(2)}) copy-start(f32[512,1]{0,1:T(1,128)S(1)} %get-tuple-element.104) | copy-start | bytes 6148
  22.2 5.8 %copy-start.39 = (f32[512,1]{0,1:T(1,128)}, f32[512,1]{0,1:T(1,128)S(1)}, u32[]{:S(2)}) copy-start(f32[512,1]{0,1:T(1,128)S(1)} %get-tuple-element.105) | copy-start | bytes 6148
  22.2 5.8 %copy-start.41 = (f32[512,1]{0,1:T(1,128)}, f32[512,1]{0,1:T(1,128)S(1)}, u32[]{:S(2)}) copy-start(f32[512,1]{0,1:T(1,128)S(1)} %get-tuple-element.106) | copy-start | bytes 6148
  22.2 5.8 %copy-start.43 = (f32[512,1]{0,1:T(1,128)}, f32[512,1]{0,1:T(1,128)S(1)}, u32[]{:S(2)}) copy-start(f32[512,1]{0,1:T(1,128)S(1)} %get-tuple-element.107) | copy-start | bytes 6148
  47.5 224.9 %all-gather.8.cloned.1.call-start = ((), (), s32[]{:S(2)}) async-start(), calls=%async_computation.2 | async-start | bytes 4866048 | tf_op jit(solution)/shard_map/all_gather | solution.py:26
  85.1 82.5 %copy-start.3 = (f32[83,6,192]{2,0,1:T(8,128)}, f32[83,6,192]{2,0,1:T(8,128)S(1)}, u32[]{:S(2)}) copy-start(f32[83,6,192]{2,0,1:T(8,128)S(1)} %reduce_sum.45) | copy-start | bytes 1147396
  157.6 10.5 %copy-start.46 = (f32[512]{0:T(512)S(1)}, f32[512]{0:T(512)}, u32[]{:S(2)}) copy-start(f32[512]{0:T(512)} %copy-done.45) | copy-start | bytes 6148
  168.6 13.3 %copy-start.1 = (bf16[1152,512]{1,0:T(8,128)(2,1)}, bf16[1152,512]{1,0:T(8,128)(2,1)S(1)}, u32[]{:S(2)}) copy-start(bf16[1152,512]{1,0:T(8,128)(2,1)S(1)} %fusion.23) | copy-start | bytes 3538948
  168.7 8.4 %collective-permute-start.2 = (bf16[512,2,192]{0,2,1:T(8,128)(2,1)S(1)}, bf16[512,2,192]{0,2,1:T(8,128)(2,1)S(1)}, u32[]{:S(2)}, u32[]{:S(2)}) collective-permute-start(bf16[512,2,192]{0,2,1:T(8,128)(2,1)S(1)} %get-tuple-element.85), channel_id=1, source_target_pairs={{0,1},{1,2},{2,3},{4,5},{5,6},{6,7},{8,9},{9,10},{10,11},{12,13},{... | collective-permute-start | bytes 1179656 | tf_op jit(solution)/shard_map/ppermute | solution.py:18
  172.4 9.6 %copy-start.12 = (f32[512,1]{0,1:T(1,128)S(1)}, f32[512,1]{0,1:T(1,128)}, u32[]{:S(2)}) copy-start(f32[512,1]{0,1:T(1,128)} %copy-done.11) | copy-start | bytes 6148
  172.4 9.6 %copy-start.14 = (f32[512,1]{0,1:T(1,128)S(1)}, f32[512,1]{0,1:T(1,128)}, u32[]{:S(2)}) copy-start(f32[512,1]{0,1:T(1,128)} %copy-done.13) | copy-start | bytes 6148
  172.4 9.6 %copy-start.16 = (f32[512,1]{0,1:T(1,128)S(1)}, f32[512,1]{0,1:T(1,128)}, u32[]{:S(2)}) copy-start(f32[512,1]{0,1:T(1,128)} %copy-done.15) | copy-start | bytes 6148
  172.4 9.6 %copy-start.18 = (f32[512,1]{0,1:T(1,128)S(1)}, f32[512,1]{0,1:T(1,128)}, u32[]{:S(2)}) copy-start(f32[512,1]{0,1:T(1,128)} %copy-done.17) | copy-start | bytes 6148
  172.4 9.6 %copy-start.20 = (f32[512,1]{0,1:T(1,128)S(1)}, f32[512,1]{0,1:T(1,128)}, u32[]{:S(2)}) copy-start(f32[512,1]{0,1:T(1,128)} %copy-done.19) | copy-start | bytes 6148
  172.4 9.6 %copy-start.22 = (f32[512,1]{0,1:T(1,128)S(1)}, f32[512,1]{0,1:T(1,128)}, u32[]{:S(2)}) copy-start(f32[512,1]{0,1:T(1,128)} %copy-done.21) | copy-start | bytes 6148
  172.4 9.6 %copy-start.24 = (f32[512,1]{0,1:T(1,128)S(1)}, f32[512,1]{0,1:T(1,128)}, u32[]{:S(2)}) copy-start(f32[512,1]{0,1:T(1,128)} %copy-done.23) | copy-start | bytes 6148
  172.4 9.6 %copy-start.26 = (f32[512,1]{0,1:T(1,128)S(1)}, f32[512,1]{0,1:T(1,128)}, u32[]{:S(2)}) copy-start(f32[512,1]{0,1:T(1,128)} %copy-done.25) | copy-start | bytes 6148
  172.4 9.6 %copy-start.28 = (f32[512,1]{0,1:T(1,128)S(1)}, f32[512,1]{0,1:T(1,128)}, u32[]{:S(2)}) copy-start(f32[512,1]{0,1:T(1,128)} %copy-done.27) | copy-start | bytes 6148
  172.4 9.6 %copy-start.30 = (f32[512,1]{0,1:T(1,128)S(1)}, f32[512,1]{0,1:T(1,128)}, u32[]{:S(2)}) copy-start(f32[512,1]{0,1:T(1,128)} %copy-done.29) | copy-start | bytes 6148
  172.5 9.6 %copy-start.32 = (f32[512,1]{0,1:T(1,128)S(1)}, f32[512,1]{0,1:T(1,128)}, u32[]{:S(2)}) copy-start(f32[512,1]{0,1:T(1,128)} %copy-done.31) | copy-start | bytes 6148
  172.5 9.6 %copy-start.34 = (f32[512,1]{0,1:T(1,128)S(1)}, f32[512,1]{0,1:T(1,128)}, u32[]{:S(2)}) copy-start(f32[512,1]{0,1:T(1,128)} %copy-done.33) | copy-start | bytes 6148
  172.5 9.6 %copy-start.36 = (f32[512,1]{0,1:T(1,128)S(1)}, f32[512,1]{0,1:T(1,128)}, u32[]{:S(2)}) copy-start(f32[512,1]{0,1:T(1,128)} %copy-done.35) | copy-start | bytes 6148
  172.5 9.6 %copy-start.38 = (f32[512,1]{0,1:T(1,128)S(1)}, f32[512,1]{0,1:T(1,128)}, u32[]{:S(2)}) copy-start(f32[512,1]{0,1:T(1,128)} %copy-done.37) | copy-start | bytes 6148
  172.5 9.6 %copy-start.40 = (f32[512,1]{0,1:T(1,128)S(1)}, f32[512,1]{0,1:T(1,128)}, u32[]{:S(2)}) copy-start(f32[512,1]{0,1:T(1,128)} %copy-done.39) | copy-start | bytes 6148
  172.5 9.6 %copy-start.42 = (f32[512,1]{0,1:T(1,128)S(1)}, f32[512,1]{0,1:T(1,128)}, u32[]{:S(2)}) copy-start(f32[512,1]{0,1:T(1,128)} %copy-done.41) | copy-start | bytes 6148
  172.5 9.6 %copy-start.44 = (f32[512,1]{0,1:T(1,128)S(1)}, f32[512,1]{0,1:T(1,128)}, u32[]{:S(2)}) copy-start(f32[512,1]{0,1:T(1,128)} %copy-done.43) | copy-start | bytes 6148
  172.5 9.1 %collective-permute-start.3 = (bf16[512,2,192]{0,2,1:T(8,128)(2,1)S(1)}, bf16[512,2,192]{0,2,1:T(8,128)(2,1)S(1)}, u32[]{:S(2)}, u32[]{:S(2)}) collective-permute-start(bf16[512,2,192]{0,2,1:T(8,128)(2,1)S(1)} %get-tuple-element.86), channel_id=1, source_target_pairs={{1,0},{2,1},{3,2},{5,4},{6,5},{7,6},{9,8},{10,9},{11,10},{13,12},{... | collective-permute-start | bytes 1179656 | tf_op jit(solution)/shard_map/ppermute | solution.py:19
  272.4 9.8 %copy-start.4 = (f32[83,6,192]{2,0,1:T(8,128)S(1)}, f32[83,6,192]{2,0,1:T(8,128)}, u32[]{:S(2)}) copy-start(f32[83,6,192]{2,0,1:T(8,128)} %copy-done.3) | copy-start | bytes 1147396
  (9 other events, 29.0 us)
Sparse Core Ops, SparseCore 0:
  9.5 72.9 all-gather.3
  84.7 72.8 all-gather.5
  200.9 71.4 all-gather.7
